TPU v7x, 512 devices: a whole 4x4x16 slice. The times are simulated.
512 devices in a mesh: tm: 64 (over x_lo, z, core), head: 8 (over x_hi, y).
Axes of the slice: x: 4 (x_hi: 2, x_lo: 2; x = x_hi * 2 + x_lo), y: 4, z: 16, core: 2. Of those that a mesh axis runs over, the one named last changes fastest.
Arguments:
- frames: bfloat16 [16384, 1280], P('tm', 'head'), may hold values from -6 to 6
- segment_ids: int32 [16384], replicated, may hold values from 0 to 127, never falling along the last dimension, each value on 1 to 256 neighbouring positions
- ln_gain: float32 [1280], replicated, may hold values from 0.5 to 1.5
- ln_bias: float32 [1280], replicated, may hold values from -1.5 to 1.5
- qkv_weight: bfloat16 [3, 1280, 1024], P(None, None, 'head'), may hold values from -3 to 3
- out_weight: bfloat16 [1024, 1280], P(None, 'head'), may hold values from -0.1875 to 0.1875
- out_bias: float32 [1280], P('head'), may hold values from -2.5 to 2.5
- adapter: bfloat16 [1280, 2560], P('head'), may hold values from -0.15625 to 0.15625
- rms_gain: float32 [2560], replicated, may hold values from 0.25 to 1.75
- x_weight: bfloat16 [2560, 2560], P(None, 'head'), may hold values from -0.125 to 0.125
- bc_weight: bfloat16 [2560, 256], P(None, 'head'), may hold values from -0.125 to 0.125
- decay: float32 [4096, 40], P('tm', 'head'), may hold values from 0 to 1
- skip_gain: float32 [40], P('head'), may hold values from 0.5 to 1.5
Outputs:
- encoded: bfloat16 [16384, 1280], P('tm', 'head')
- mixed: bfloat16 [4096, 2560], P('tm', 'head')
Inputs may be any that keep to these rules, and one draw needn't show every extreme that they name: `segment_ids`: segment numbers never fall along the frames; each segment holds 1 to 256 frames and one holds exactly 256.
All inputs are finite; a program needn't handle non-finite values.
Results may differ from a plain program's by a relative error of at most 0.008.
Values may be sent and summed in bfloat16 or wider, within the bound.
No kernel may reach another device: no remote copies, remote signals or barrier semaphores. Data moves between devices by JAX's collectives and lax.ppermute only.
A program may use at most 64 MiB of HBM per device.

v0:
```python
import math
import jax
import jax.numpy as jnp
from jax import lax
from jax.sharding import PartitionSpec as P

EHEAD_DIM = 64
HDIM = 64
NSTATE = 128
WINDOW = 256
EPSILON = 1e-05
HIGHEST = lax.Precision.HIGHEST


def with_halo(block, sides, width):
    for axis, dim in sides:
        count = lax.axis_size(axis)
        forward = [(i, i + 1) for i in range(count - 1)]
        backward = [(target, source) for source, target in forward]
        low = lax.ppermute(
            lax.slice_in_dim(block, block.shape[dim] - width, None, axis=dim), axis, forward
        )
        high = lax.ppermute(lax.slice_in_dim(block, 0, width, axis=dim), axis, backward)
        block = jnp.concatenate([low, block, high], axis=dim)
    return block


def prefix(part, axis, combine, identity):
    place = lax.axis_index(axis)
    gathered = jax.tree.map(lambda a: lax.all_gather(a, axis), part)
    state = jax.tree.map(lambda a, e: jnp.zeros_like(a) + jnp.asarray(e, a.dtype), part, identity)

    def one(hop, state):
        return combine(
            state, jax.tree.map(lambda a: lax.dynamic_index_in_dim(a, hop, 0, False), gathered)
        )

    return lax.fori_loop(0, place, one, state)


def layer_norm(values, gain, offset):
    center_mean = jnp.mean(values, axis=-1, keepdims=True)
    spread = jnp.mean(jnp.square(values - center_mean), axis=-1, keepdims=True)
    return (values - center_mean) * lax.rsqrt(spread + EPSILON) * gain + offset


def block_terms(inputs, b_in, c_in, decay):
    log_decay = jnp.log(decay)
    cumulative = jnp.cumsum(log_decay, axis=0)
    length = inputs.shape[0]
    sequence_indices = jnp.arange(length, dtype=jnp.int32)
    causal = sequence_indices[:, None] >= sequence_indices[None, :]
    log_gap = cumulative[:, None, :] - cumulative[None, :, :]
    weights = jnp.exp(jnp.where(causal[:, :, None], log_gap, -1e30))
    driven = inputs * (1.0 - decay)[:, :, None]
    affinity = jnp.dot(c_in, b_in.T, preferred_element_type=jnp.float32)
    within = jnp.einsum("tsh,shp->thp", affinity[:, :, None] * weights, driven, precision=HIGHEST)
    tail_decay = jnp.exp(cumulative[-1][None, :] - cumulative)
    end_state = jnp.einsum(
        "sh,shp,sn->hpn", tail_decay, driven, b_in.astype(jnp.float32), precision=HIGHEST
    )
    return (within, jnp.exp(cumulative), jnp.exp(cumulative[-1]), end_state)


def combine_states(earlier, later):
    return (earlier[0] * later[0], later[0][:, None, None] * earlier[1] + later[1])


def per_device(
    frames,
    segment_ids,
    ln_gain,
    ln_bias,
    qkv_weight,
    out_weight,
    out_bias,
    adapter,
    rms_gain,
    x_weight,
    bc_weight,
    decay,
    skip_gain,
):
    frame_count = frames.shape[0]
    margin = WINDOW
    tm_slot = lax.axis_index("tm")
    gathered = lax.all_gather(frames, "head", axis=1, tiled=True)
    normed = layer_norm(gathered.astype(jnp.float32), ln_gain, ln_bias).astype(jnp.bfloat16)
    queries = jnp.dot(normed, qkv_weight[0], preferred_element_type=jnp.float32).astype(
        jnp.bfloat16
    )
    keys_own = jnp.dot(normed, qkv_weight[1], preferred_element_type=jnp.float32).astype(
        jnp.bfloat16
    )
    values_own = jnp.dot(normed, qkv_weight[2], preferred_element_type=jnp.float32).astype(
        jnp.bfloat16
    )
    joined = jnp.concatenate([keys_own, values_own], axis=1)
    extended = with_halo(joined, (("tm", 0),), margin)
    head_width = keys_own.shape[1]
    keys_ext = extended[:, :head_width]
    values_ext = extended[:, head_width:]
    ids_pad = jnp.pad(segment_ids, (margin, margin), constant_values=-1)
    local_ids = lax.dynamic_slice_in_dim(
        ids_pad, tm_slot * frame_count, frame_count + 2 * margin, 0
    )
    heads_dev = queries.shape[1] // EHEAD_DIM
    qblock = math.gcd(frame_count, 512)
    span_rows = qblock + 2 * margin

    def attend(block_index):
        begin = block_index * qblock
        query_rows = queries.reshape(qblock, heads_dev, EHEAD_DIM)
        key_rows = keys_ext.reshape(span_rows, heads_dev, EHEAD_DIM)
        value_rows = values_ext.reshape(span_rows, heads_dev, EHEAD_DIM)
        query_ids = lax.dynamic_slice_in_dim(local_ids, begin + margin, qblock, 0)
        scores = jnp.einsum(
            "qhe,khe->hqk", query_rows, key_rows, preferred_element_type=jnp.float32
        ) * EHEAD_DIM ** (-0.5)
        allowed = query_ids[:, None] == local_ids[None, :]
        scores = jnp.where(allowed[None], scores, -1e30)
        peak = jnp.max(scores, axis=-1, keepdims=True)
        raised = jnp.exp(scores - peak)
        probs = (raised / jnp.sum(raised, axis=-1, keepdims=True)).astype(jnp.bfloat16)
        blended = jnp.einsum("hqk,khe->qhe", probs, value_rows, preferred_element_type=jnp.float32)
        return blended.astype(jnp.bfloat16).reshape(qblock, heads_dev * EHEAD_DIM)

    attended = lax.map(attend, jnp.arange(frame_count // qblock, dtype=jnp.int32)).reshape(
        frame_count, heads_dev * EHEAD_DIM
    )
    attention = jnp.dot(
        lax.all_gather(attended, "head", axis=1, tiled=True),
        out_weight,
        preferred_element_type=jnp.float32,
    )
    encoded = (frames.astype(jnp.float32) + attention + out_bias).astype(jnp.bfloat16)
    pooled = jnp.mean(
        encoded.astype(jnp.float32).reshape(frame_count // 4, 4, encoded.shape[1]), axis=1
    ).astype(jnp.bfloat16)
    partial_sum = jnp.dot(pooled, adapter, preferred_element_type=jnp.float32)
    projected = lax.psum(partial_sum, "head")
    scaled = (
        projected
        * lax.rsqrt(jnp.mean(jnp.square(projected), axis=1, keepdims=True) + EPSILON)
        * rms_gain
    ).astype(jnp.bfloat16)
    inputs = jax.nn.silu(jnp.dot(scaled, x_weight, preferred_element_type=jnp.float32)).astype(
        jnp.bfloat16
    )
    coupler_part = jax.nn.silu(
        jnp.dot(scaled, bc_weight, preferred_element_type=jnp.float32)
    ).astype(jnp.bfloat16)
    couplers = lax.all_gather(coupler_part, "head", axis=1, tiled=True)
    token_count = inputs.shape[0]
    state_heads = inputs.shape[1] // HDIM
    inputs_wide = inputs.astype(jnp.float32).reshape(token_count, state_heads, HDIM)
    c_rows = couplers[:, NSTATE:]
    within, growth, total_decay, end_state = block_terms(
        inputs_wide, couplers[:, :NSTATE], c_rows, decay
    )
    identity = (jnp.ones_like(total_decay), jnp.zeros_like(end_state))
    incoming = prefix((total_decay, end_state), "tm", combine_states, identity)
    from_state = jnp.einsum(
        "tn,hpn->thp", c_rows.astype(jnp.float32), incoming[1], precision=HIGHEST
    )
    result_rows = within + growth[:, :, None] * from_state + skip_gain[None, :, None] * inputs_wide
    mixed = result_rows.astype(jnp.bfloat16).reshape(token_count, state_heads * HDIM)
    return (encoded, mixed)


def solution(mesh):
    placed = (
        P("tm", "head"),
        P(),
        P(),
        P(),
        P(None, None, "head"),
        P(None, "head"),
        P("head"),
        P("head", None),
        P(),
        P(None, "head"),
        P(None, "head"),
        P("tm", "head"),
        P("head"),
    )
    return jax.shard_map(
        per_device,
        mesh=mesh,
        in_specs=placed,
        out_specs=(P("tm", "head"), P("tm", "head")),
        check_vma=False,
    )
```

profile of v0, /device:TPU:483, one launch (start us, length us, event | category | flops | bytes accessed | tf_op | source)
XLA Modules:
  0.0 432.9 jit_solution(7128152274875315925)
XLA Ops:
  7.3 29.6 %all_gather.19 = bf16[256,1280]{0,1:T(8,128)(2,1)S(1)} all-gather(bf16[256,160]{0,1:T(8,128)(2,1)} %param.15), channel_id=1, replica_groups=mesh['tm'=64,'head'=8] {'head'}, dimensions={1}, use_global_device_ids=true | all-gather | bytes 737280 | tf_op jit(solution)/shard_map/all_gather | solution.py:87
  38.4 8.7 %collective-permute-start.1 = (bf16[256,256]{0,1:T(8,128)(2,1)S(1)}, bf16[256,256]{0,1:T(8,128)(2,1)S(1)}, u32[]{:S(2)}, u32[]{:S(2)}) collective-permute-start(bf16[256,256]{0,1:T(8,128)(2,1)S(1)} %pad_maximum_fusion.1), channel_id=1, source_target_pairs={{8,0},{16,8},{24,16},{32,24},{40,32},{48,40},{56,48},{64,56},{72,6... | collective-permute-start | bytes 393224 | tf_op jit(solution)/shard_map/ppermute | solution.py:23
  47.1 1.3 collective-permute-start
  49.1 1.2 collective-permute-done
  52.2 29.1 %all_gather.20 = bf16[256,1024]{0,1:T(8,128)(2,1)S(1)} all-gather(bf16[256,128]{0,1:T(8,128)(2,1)S(1)} %bitcast.65), channel_id=1, replica_groups=mesh['tm'=64,'head'=8] {'head'}, dimensions={1}, use_global_device_ids=true | all-gather | bytes 589824 | tf_op jit(solution)/shard_map/all_gather | solution.py:132
  82.1 1.1 fusion.37
  83.6 103.0 %all-reduce.3.cloned.1.call-done = f32[64,2560]{1,0:T(8,128)} async-done(((f32[64,2560]{1,0:T(8,128)}), f32[64,2560]{1,0:T(8,128)}) %all-reduce.3.cloned.1.call-update) | async-done | bytes 655376 | tf_op jit(solution)/shard_map/psum | solution.py:141
  186.6 1.3 multiply_reduce_fusion
  188.0 1.4 multiply_convert_fusion.4
  189.4 28.0 %all_gather.21 = bf16[64,256]{0,1:T(8,128)(2,1)S(1)} all-gather(bf16[64,32]{0,1:T(8,128)(2,1)S(1)} %multiply_convert_fusion.4), channel_id=1, replica_groups=mesh['tm'=64,'head'=8] {'head'}, dimensions={1}, use_global_device_ids=true | all-gather | bytes 36864 | tf_op jit(solution)/shard_map/all_gather | solution.py:153
  219.2 71.0 %all-gather.1 = f32[64,1,5]{2,1,0:T(1,128)S(1)} all-gather(f32[1,1,5]{2,1,0:T(1,128)S(1)} %get-tuple-element.86), channel_id=1, replica_groups=mesh['tm'=64,'head'=8] {'tm'}, dimensions={0}, use_global_device_ids=true | all-gather | bytes 1300 | tf_op jit(solution)/shard_map/all_gather | solution.py:30
  290.4 67.9 %all-gather.4.cloned.1.call-done = f32[320,64,128]{2,1,0:T(8,128)} async-done(((f32[5,64,128]{2,1,0:T(8,128)}), f32[320,64,128]{2,1,0:T(8,128)}) %all-gather.4.cloned.1.call-update) | async-done | bytes 10485776 | tf_op jit(solution)/shard_map/all_gather | solution.py:30
  358.3 66.4 %while.3 = (s32[]{:T(128)}, f32[5,64,128]{2,1,0:T(8,128)S(1)}, s32[]{:T(128)}, f32[64,5]{1,0:T(8,128)S(1)}, f32[64,5,64,128]{3,2,1,0:T(8,128)}, /*index=5*/s32[]{:T(128)}, s32[]{:T(128)}, s32[]{:T(128)}) while((s32[]{:T(128)}, f32[5,64,128]{2,1,0:T(8,128)S(1)}, s32[]{:T(128)}, f32[64,5]{1,0:T(8,128)S(1)}, f32[64,5,64,128]{3,2,1,0:T(8,128)}, ...), condition=%wide.region_9.10_spmd, body=%wide.region_8.9_spmd.sunk | while | flops 81925 | bytes 491715 | solution.py:38
  358.3 1.0 bitcast_add_fusion.2
  359.4 1.0 bitcast_add_fusion.2
  360.5 1.0 bitcast_add_fusion.2
  361.5 1.0 bitcast_add_fusion.2
  362.6 1.0 bitcast_add_fusion.2
  364.7 1.0 bitcast_add_fusion.2
  365.7 1.0 bitcast_add_fusion.2
  366.8 1.0 bitcast_add_fusion.2
  367.8 1.0 bitcast_add_fusion.2
  368.9 1.0 bitcast_add_fusion.2
  369.9 1.0 bitcast_add_fusion.2
  371.0 1.0 bitcast_add_fusion.2
  372.0 1.0 bitcast_add_fusion.2
  374.1 1.0 bitcast_add_fusion.2
  375.2 1.0 bitcast_add_fusion.2
  376.3 1.0 bitcast_add_fusion.2
  377.3 1.0 bitcast_add_fusion.2
  378.4 1.0 bitcast_add_fusion.2
  379.4 1.0 bitcast_add_fusion.2
  (180 shorter events, 53.7 us)
Async XLA Ops:
  7.2 210.2 %copy-start = (bf16[2560,320]{0,1:T(8,128)(2,1)S(1)}, bf16[2560,320]{0,1:T(8,128)(2,1)}, u32[]{:S(2)}) copy-start(bf16[2560,320]{0,1:T(8,128)(2,1)} %param.24) | copy-start | bytes 4915204
  7.2 30.1 %copy-start.9 = (f32[1280]{0:T(1024)S(1)}, f32[1280]{0:T(1024)}, u32[]{:S(2)}) copy-start(f32[1280]{0:T(1024)} %param.18) | copy-start | bytes 15364
  7.2 30.1 %copy-start.10 = (f32[1280]{0:T(1024)S(1)}, f32[1280]{0:T(1024)}, u32[]{:S(2)}) copy-start(f32[1280]{0:T(1024)} %param.17) | copy-start | bytes 15364
  7.2 30.5 %copy-start.14 = (bf16[3,1280,128]{2,1,0:T(8,128)(2,1)S(1)}, bf16[3,1280,128]{2,1,0:T(8,128)(2,1)}, u32[]{:S(2)}) copy-start(bf16[3,1280,128]{2,1,0:T(8,128)(2,1)} %param.19) | copy-start | bytes 2949124
  7.2 179.4 %all-reduce.3.cloned.1.call-start = ((), (), s32[]{:S(2)}) async-start(), calls=%async_computation | async-start | bytes 1310720 | tf_op jit(solution)/shard_map/psum | solution.py:141
  38.1 10.7 %copy-start.6 = (s32[16384]{0:T(1024)S(1)}, s32[16384]{0:T(1024)}, u32[]{:S(2)}) copy-start(s32[16384]{0:T(1024)} %param.16) | copy-start | bytes 196612
  38.4 10.7 %collective-permute-start.1 = (bf16[256,256]{0,1:T(8,128)(2,1)S(1)}, bf16[256,256]{0,1:T(8,128)(2,1)S(1)}, u32[]{:S(2)}, u32[]{:S(2)}) collective-permute-start(bf16[256,256]{0,1:T(8,128)(2,1)S(1)} %pad_maximum_fusion.1), channel_id=1, source_target_pairs={{8,0},{16,8},{24,16},{32,24},{40,32},{48,40},{56,48},{64,56},{72,6... | collective-permute-start | bytes 393224 | tf_op jit(solution)/shard_map/ppermute | solution.py:23
  47.1 3.2 collective-permute-start
  51.2 30.2 %copy-start.4 = (bf16[1024,160]{0,1:T(8,128)(2,1)S(1)}, bf16[1024,160]{0,1:T(8,128)(2,1)}, u32[]{:S(2)}) copy-start(bf16[1024,160]{0,1:T(8,128)(2,1)} %param.20) | copy-start | bytes 983044
  51.2 30.2 %copy-start.5 = (bf16[256,160]{0,1:T(8,128)(2,1)S(1)}, bf16[256,160]{0,1:T(8,128)(2,1)}, u32[]{:S(2)}) copy-start(bf16[256,160]{0,1:T(8,128)(2,1)} %param.15) | copy-start | bytes 245764
  51.2 30.2 %copy-start.12 = (f32[160]{0:T(256)S(1)}, f32[160]{0:T(256)}, u32[]{:S(2)}) copy-start(f32[160]{0:T(256)} %param.21) | copy-start | bytes 1924
  52.2 29.8 %copy-start.2 = (bf16[160,2560]{1,0:T(8,128)(2,1)S(1)}, bf16[160,2560]{1,0:T(8,128)(2,1)}, u32[]{:S(2)}) copy-start(bf16[160,2560]{1,0:T(8,128)(2,1)} %param.22) | copy-start | bytes 2457604
  81.7 1.6 copy-start.3
  81.8 1.5 copy-start.11
  82.1 105.9 %copy-start.7 = (bf16[2560,32]{0,1:T(8,128)(2,1)S(1)}, bf16[2560,32]{0,1:T(8,128)(2,1)}, u32[]{:S(2)}) copy-start(bf16[2560,32]{0,1:T(8,128)(2,1)} %param.25) | copy-start | bytes 491524
  82.1 105.9 %copy-start.8 = (f32[2560]{0:T(1024)S(1)}, f32[2560]{0:T(1024)}, u32[]{:S(2)}) copy-start(f32[2560]{0:T(1024)} %param.23) | copy-start | bytes 30724
  83.2 275.1 %all-gather.4.cloned.1.call-start = ((), (), s32[]{:S(2)}) async-start(), calls=%async_computation.1 | async-start | bytes 10649600 | tf_op jit(solution)/shard_map/all_gather | solution.py:30
  186.6 30.8 %copy-start.1 = (f32[64,2560]{1,0:T(8,128)S(1)}, f32[64,2560]{1,0:T(8,128)}, u32[]{:S(2)}) copy-start(f32[64,2560]{1,0:T(8,128)} %all-reduce.3.cloned.1.call-done) | copy-start | bytes 1966084
  358.3 66.6 %copy-start.13 = (f32[5]{0:T(128)S(1)}, f32[5]{0:T(128)}, u32[]{:S(2)}) copy-start(f32[5]{0:T(128)} %param.27) | copy-start | bytes 64
Sparse Core Ops, SparseCore 0:
  83.3 103.2 all-reduce.2
  219.2 139.0 all-gather.3
where the time goes:
time: 435 us; the launch traced here: 433 us
  waiting for transfers between devices  172 us (40%)
  blocking collectives  158 us (36%)
  other arithmetic  66.5 us (15%)
  between operations  14.4 us (3%)
  starting transfers between devices  10.1 us (2%)
  matrix products  7.89 us (2%)
    psum x1, waiting for transfers between devices, per_device(): projected = lax.psum(partial_sum, 'head')  103 us
    all_gather x1, blocking collectives, prefix(): gathered = jax.tree.map(lambda a: lax.all_gather(a, axis), part)  71 us
    all_gather x1, waiting for transfers between devices, prefix(): gathered = jax.tree.map(lambda a: lax.all_gather(a, axis), part)  67.9 us
    add x63, other arithmetic, combine_states(): later[0][:, None, None] * earlier[1] + later[1]  63.8 us
    all_gather x1, blocking collectives, per_device(): gathered = lax.all_gather(frames, 'head', axis=1, tiled=True)  29.6 us
    all_gather x1, blocking collectives, per_device(): lax.all_gather(attended, 'head', axis=1, tiled=True)  29.1 us
    all_gather x1, blocking collectives, per_device(): couplers = lax.all_gather(coupler_part, 'head', axis=1, tiled=True)  28 us
  transfers between devices with their start and end apart: 4, of which 3 were waited for; matrix products, arithmetic and copies ran while one was open for 0% of the time, Pallas kernels for 0%

commit v1 on v0

--- a/solution.py
+++ b/solution.py
@@ -84,7 +84,9 @@
     frame_count = frames.shape[0]
     margin = WINDOW
     tm_slot = lax.axis_index("tm")
-    gathered = lax.all_gather(frames, "head", axis=1, tiled=True)
+    gathered = jnp.concatenate(
+        lax.all_to_all(jnp.stack([frames for _ in range(lax.axis_size("head"))]), "head", 0, 0), 1
+    )
     normed = layer_norm(gathered.astype(jnp.float32), ln_gain, ln_bias).astype(jnp.bfloat16)
     queries = jnp.dot(normed, qkv_weight[0], preferred_element_type=jnp.float32).astype(
         jnp.bfloat16

time: 435 us -> 417 us (0.959)
  the two profiles are of different devices: /device:TPU:483 before, /device:TPU:487 now
where the time goes in v1:
time: 417 us; the launch traced here: 415 us
  waiting for transfers between devices  181 us (43%)
  blocking collectives  128 us (31%)
  other arithmetic  66.5 us (16%)
  between operations  14.4 us (3%)
  starting transfers between devices  10.9 us (3%)
  matrix products  7.86 us (2%)
  local copies, waits for them, and re-layouts  4.25 us (1%)
    psum x1, waiting for transfers between devices, per_device(): projected = lax.psum(partial_sum, 'head')  101 us
    all_gather x1, blocking collectives, prefix(): gathered = jax.tree.map(lambda a: lax.all_gather(a, axis), part)  70.7 us
    all_gather x1, waiting for transfers between devices, prefix(): gathered = jax.tree.map(lambda a: lax.all_gather(a, axis), part)  68.4 us
    add x63, other arithmetic, combine_states(): later[0][:, None, None] * earlier[1] + later[1]  63.8 us
    all_gather x1, blocking collectives, per_device(): lax.all_gather(attended, 'head', axis=1, tiled=True)  29.5 us
    all_gather x1, blocking collectives, per_device(): couplers = lax.all_gather(coupler_part, 'head', axis=1, tiled=True)  27.8 us
    all_to_all x1, waiting for transfers between devices, per_device(): lax.all_to_all(jnp.stack([frames for _ in range(lax.axis_size('head'))]),...  9.97 us
  transfers between devices with their start and end apart: 5, of which 4 were waited for; matrix products, arithmetic and copies ran while one was open for 0% of the time, Pallas kernels for 0%

profile of v1, /device:TPU:487, one launch (start us, length us, event | category | flops | bytes accessed | tf_op | source)
XLA Modules:
  0.0 414.9 jit_solution(17677580264237363090)
XLA Ops:
  7.2 1.9 stack.2
  9.1 6.9 %all-to-all-start = ((bf16[8,256,160]{1,2,0:T(8,128)(2,1)}), bf16[8,256,160]{1,2,0:T(8,128)(2,1)S(1)}, u32[]{:S(2)}, u32[]{:S(2)}) async-start(bf16[8,256,160]{1,2,0:T(8,128)(2,1)} %stack.2), calls=%async_computation | async-start | bytes 1310720 | tf_op jit(solution)/shard_map/all_to_all | solution.py:88
  16.5 10.0 %all-to-all-done = bf16[8,256,160]{1,2,0:T(8,128)(2,1)S(1)} async-done(((bf16[8,256,160]{1,2,0:T(8,128)(2,1)}), bf16[8,256,160]{1,2,0:T(8,128)(2,1)S(1)}, u32[]{:S(2)}, u32[]{:S(2)}) %all-to-all-start) | async-done | bytes 655392 | tf_op jit(solution)/shard_map/all_to_all | solution.py:88
  28.0 2.7 collective-permute-start.1
  30.7 1.3 collective-permute-start
  32.3 1.6 collective-permute-done
  35.8 29.5 %all_gather.16 = bf16[256,1024]{0,1:T(8,128)(2,1)S(1)} all-gather(bf16[256,128]{0,1:T(8,128)(2,1)S(1)} %bitcast.71), channel_id=1, replica_groups=mesh['tm'=64,'head'=8] {'head'}, dimensions={1}, use_global_device_ids=true | all-gather | bytes 589824 | tf_op jit(solution)/shard_map/all_gather | solution.py:134
  66.0 1.1 fusion.37
  67.5 101.0 %all-reduce.3.cloned.1.call-done = f32[64,2560]{1,0:T(8,128)} async-done(((f32[64,2560]{1,0:T(8,128)}), f32[64,2560]{1,0:T(8,128)}) %all-reduce.3.cloned.1.call-update) | async-done | bytes 655376 | tf_op jit(solution)/shard_map/psum | solution.py:143
  168.5 1.3 multiply_reduce_fusion
  169.8 1.4 multiply_convert_fusion.4
  171.2 27.8 %all_gather.17 = bf16[64,256]{0,1:T(8,128)(2,1)S(1)} all-gather(bf16[64,32]{0,1:T(8,128)(2,1)S(1)} %multiply_convert_fusion.4), channel_id=1, replica_groups=mesh['tm'=64,'head'=8] {'head'}, dimensions={1}, use_global_device_ids=true | all-gather | bytes 36864 | tf_op jit(solution)/shard_map/all_gather | solution.py:155
  200.9 70.7 %all-gather.1 = f32[64,1,5]{2,1,0:T(1,128)S(1)} all-gather(f32[1,1,5]{2,1,0:T(1,128)S(1)} %get-tuple-element.86), channel_id=1, replica_groups=mesh['tm'=64,'head'=8] {'tm'}, dimensions={0}, use_global_device_ids=true | all-gather | bytes 1300 | tf_op jit(solution)/shard_map/all_gather | solution.py:30
  271.8 68.4 %all-gather.4.cloned.1.call-done = f32[320,64,128]{2,1,0:T(8,128)} async-done(((f32[5,64,128]{2,1,0:T(8,128)}), f32[320,64,128]{2,1,0:T(8,128)}) %all-gather.4.cloned.1.call-update) | async-done | bytes 10485776 | tf_op jit(solution)/shard_map/all_gather | solution.py:30
  340.2 66.4 %while.3 = (s32[]{:T(128)}, f32[5,64,128]{2,1,0:T(8,128)S(1)}, s32[]{:T(128)}, f32[64,5]{1,0:T(8,128)S(1)}, f32[64,5,64,128]{3,2,1,0:T(8,128)}, /*index=5*/s32[]{:T(128)}, s32[]{:T(128)}, s32[]{:T(128)}) while((s32[]{:T(128)}, f32[5,64,128]{2,1,0:T(8,128)S(1)}, s32[]{:T(128)}, f32[64,5]{1,0:T(8,128)S(1)}, f32[64,5,64,128]{3,2,1,0:T(8,128)}, ...), condition=%wide.region_9.10_spmd, body=%wide.region_8.9_spmd.sunk | while | flops 81925 | bytes 491715 | solution.py:38
  340.3 1.0 bitcast_add_fusion.2
  341.3 1.0 bitcast_add_fusion.2
  342.4 1.0 bitcast_add_fusion.2
  343.4 1.0 bitcast_add_fusion.2
  344.5 1.0 bitcast_add_fusion.2
  346.6 1.0 bitcast_add_fusion.2
  347.6 1.0 bitcast_add_fusion.2
  348.7 1.0 bitcast_add_fusion.2
  349.8 1.0 bitcast_add_fusion.2
  350.8 1.0 bitcast_add_fusion.2
  351.9 1.0 bitcast_add_fusion.2
  352.9 1.0 bitcast_add_fusion.2
  354.0 1.0 bitcast_add_fusion.2
  355.0 1.0 bitcast_add_fusion.2
  357.1 1.0 bitcast_add_fusion.2
  358.2 1.0 bitcast_add_fusion.2
  359.2 1.0 bitcast_add_fusion.2
  (184 shorter events, 55.8 us)
Async XLA Ops:
  7.2 191.9 %copy-start = (bf16[2560,320]{0,1:T(8,128)(2,1)S(1)}, bf16[2560,320]{0,1:T(8,128)(2,1)}, u32[]{:S(2)}) copy-start(bf16[2560,320]{0,1:T(8,128)(2,1)} %param.24) | copy-start | bytes 4915204
  7.2 8.8 %copy-start.9 = (f32[1280]{0:T(1024)S(1)}, f32[1280]{0:T(1024)}, u32[]{:S(2)}) copy-start(f32[1280]{0:T(1024)} %param.17) | copy-start | bytes 15364
  7.2 8.9 %copy-start.10 = (f32[1280]{0:T(1024)S(1)}, f32[1280]{0:T(1024)}, u32[]{:S(2)}) copy-start(f32[1280]{0:T(1024)} %param.18) | copy-start | bytes 15364
  7.2 8.9 %copy-start.6 = (s32[16384]{0:T(1024)S(1)}, s32[16384]{0:T(1024)}, u32[]{:S(2)}) copy-start(s32[16384]{0:T(1024)} %param.16) | copy-start | bytes 196612
  9.1 17.3 %all-to-all-start = ((bf16[8,256,160]{1,2,0:T(8,128)(2,1)}), bf16[8,256,160]{1,2,0:T(8,128)(2,1)S(1)}, u32[]{:S(2)}, u32[]{:S(2)}) async-start(bf16[8,256,160]{1,2,0:T(8,128)(2,1)} %stack.2), calls=%async_computation | async-start | bytes 1310720 | tf_op jit(solution)/shard_map/all_to_all | solution.py:88
  16.0 11.3 %copy-start.14 = (bf16[3,1280,128]{2,1,0:T(8,128)(2,1)S(1)}, bf16[3,1280,128]{2,1,0:T(8,128)(2,1)}, u32[]{:S(2)}) copy-start(bf16[3,1280,128]{2,1,0:T(8,128)(2,1)} %param.19) | copy-start | bytes 2949124
  16.0 152.5 %all-reduce.3.cloned.1.call-start = ((), (), s32[]{:S(2)}) async-start(), calls=%async_computation.1 | async-start | bytes 1310720 | tf_op jit(solution)/shard_map/psum | solution.py:143
  28.0 4.3 %collective-permute-start.1 = (bf16[256,256]{0,1:T(8,128)(2,1)S(1)}, bf16[256,256]{0,1:T(8,128)(2,1)S(1)}, u32[]{:S(2)}, u32[]{:S(2)}) collective-permute-start(bf16[256,256]{0,1:T(8,128)(2,1)S(1)} %pad_maximum_fusion.1), channel_id=1, source_target_pairs={{8,0},{16,8},{24,16},{32,24},{40,32},{48,40},{56,48},{64,56},{72,6... | collective-permute-start | bytes 393224 | tf_op jit(solution)/shard_map/ppermute | solution.py:23
  30.7 3.2 collective-permute-start
  34.8 30.5 %copy-start.4 = (bf16[1024,160]{0,1:T(8,128)(2,1)S(1)}, bf16[1024,160]{0,1:T(8,128)(2,1)}, u32[]{:S(2)}) copy-start(bf16[1024,160]{0,1:T(8,128)(2,1)} %param.20) | copy-start | bytes 983044
  34.8 30.5 %copy-start.5 = (bf16[256,160]{0,1:T(8,128)(2,1)S(1)}, bf16[256,160]{0,1:T(8,128)(2,1)}, u32[]{:S(2)}) copy-start(bf16[256,160]{0,1:T(8,128)(2,1)} %param.15) | copy-start | bytes 245764
  34.8 30.5 %copy-start.12 = (f32[160]{0:T(256)S(1)}, f32[160]{0:T(256)}, u32[]{:S(2)}) copy-start(f32[160]{0:T(256)} %param.21) | copy-start | bytes 1924
  35.8 30.2 %copy-start.2 = (bf16[160,2560]{1,0:T(8,128)(2,1)S(1)}, bf16[160,2560]{1,0:T(8,128)(2,1)}, u32[]{:S(2)}) copy-start(bf16[160,2560]{1,0:T(8,128)(2,1)} %param.22) | copy-start | bytes 2457604
  65.6 1.5 copy-start.3
  65.7 1.5 copy-start.11
  66.0 103.8 %copy-start.7 = (bf16[2560,32]{0,1:T(8,128)(2,1)S(1)}, bf16[2560,32]{0,1:T(8,128)(2,1)}, u32[]{:S(2)}) copy-start(bf16[2560,32]{0,1:T(8,128)(2,1)} %param.25) | copy-start | bytes 491524
  66.0 103.8 %copy-start.8 = (f32[2560]{0:T(1024)S(1)}, f32[2560]{0:T(1024)}, u32[]{:S(2)}) copy-start(f32[2560]{0:T(1024)} %param.23) | copy-start | bytes 30724
  67.1 273.1 %all-gather.4.cloned.1.call-start = ((), (), s32[]{:S(2)}) async-start(), calls=%async_computation.2 | async-start | bytes 10649600 | tf_op jit(solution)/shard_map/all_gather | solution.py:30
  168.5 30.6 %copy-start.1 = (f32[64,2560]{1,0:T(8,128)S(1)}, f32[64,2560]{1,0:T(8,128)}, u32[]{:S(2)}) copy-start(f32[64,2560]{1,0:T(8,128)} %all-reduce.3.cloned.1.call-done) | copy-start | bytes 1966084
  340.2 66.6 %copy-start.13 = (f32[5]{0:T(128)S(1)}, f32[5]{0:T(128)}, u32[]{:S(2)}) copy-start(f32[5]{0:T(128)} %param.27) | copy-start | bytes 64
Sparse Core Ops, SparseCore 0:
  67.2 101.2 all-reduce.2
  200.9 139.3 all-gather.3
